TPU v7x, 256 devices: a whole 4x4x8 slice. The times are simulated.
256 devices in a mesh: grp: 8 (over y, core), dom: 32 (over x, z).
Axes of the slice: x: 4, y: 4, z: 8, core: 2. Of those that a mesh axis runs over, the one named last changes fastest.
Arguments:
- fine_nodes: bfloat16 [8, 24576, 128], P('grp', 'dom'), may hold values from -6 to 6
- fine_edges: bfloat16 [8, 294912, 128], P('grp', 'dom'), may hold values from -6 to 6
- fine_senders: int32 [8, 294912], P('grp', 'dom'), may hold values from 0 to 1535
- fine_receivers: int32 [8, 294912], P('grp', 'dom'), may hold values from 0 to 767, as said below
- edge_count: int32 [8, 32], P('grp', 'dom'), may hold values from 4608 to 9216, as said below
- ghost_send: int32 [8, 1024, 24], P('grp', 'dom'), may hold values from 0 to 767
- fine_parent: int32 [8, 24576], P('grp', 'dom'), may hold values from 0 to 16383, as said below
- coarse_nodes: bfloat16 [16384, 128], P('dom'), may hold values from -6 to 6
- coarse_edges: bfloat16 [131072, 128], P('dom'), may hold values from -6 to 6
- coarse_senders: int32 [131072], P('dom'), may hold values from 0 to 16383
- coarse_receivers: int32 [131072], P('dom'), may hold values from 0 to 511, as said below
- edge_in: bfloat16 [2, 384, 128], replicated, may hold values from -0.3125 to 0.3125
- node_in: bfloat16 [3, 256, 128], replicated, may hold values from -0.375 to 0.375
- mlp_out: bfloat16 [5, 128, 128], replicated, may hold values from -0.5 to 0.5
Outputs:
- fine_out: bfloat16 [8, 24576, 128], P('grp', 'dom')
- coarse_out: bfloat16 [16384, 128], P('dom')
Inputs may be any that keep to these rules, and one draw needn't show every extreme that they name: `edge_count`: each device's live edge slot count; slots from that count on are padding; 9216 on at least one device. `fine_receivers`: nondecreasing along each device's 9216 slots; padding slots hold 767. `fine_senders`: below 768: a local node; 768 + s * 24 + k: ghost slot k received from dom index s of the same slab. `ghost_send`: local node indices; row p of a device's block lists the nodes sent to dom index p. `fine_parent`: global coarse index; owner o holds coarse nodes o * 512 to (o + 1) * 512 - 1. Most parents of a fine node of dom index d are owned by d itself; the others may be owned by any owner. `coarse_senders`: global coarse index of the sender. `coarse_receivers`: nondecreasing within each owner's 4096 edges.
All inputs are finite; a program needn't handle non-finite values.
Results may differ from a plain program's by a relative error of at most 0.015.
Values may be sent and summed in bfloat16 or wider, within the bound.
A program may use at most 64 MiB of HBM per device.

v0:
```python
import math

import jax
import jax.numpy as jnp
from jax import lax
from jax.sharding import Mesh
from jax.sharding import PartitionSpec as P

DOM = ("dom_0", "dom_1")


def in_blocks(array, dim, peers):
    shape = array.shape
    blocks = array.reshape(*shape[:dim], peers, shape[dim] // peers, *shape[dim + 1 :])
    return jnp.moveaxis(blocks, dim, 0)


def summed_on_arrival(array, axis, dim):
    peers = lax.axis_size(axis)
    blocks = lax.all_to_all(in_blocks(array, dim, peers), axis, 0, 0, tiled=True)
    return jnp.sum(blocks.astype(jnp.float32), axis=0)


def side_by_side(arrays, axis, dim, along):
    widths = [math.prod(a.shape[along:]) for a in arrays]
    both = jnp.concatenate(
        [a.reshape(*a.shape[:along], w) for a, w in zip(arrays, widths)], axis=along
    )
    out = summed_on_arrival(both, axis, dim)
    blocks = jnp.split(out, [sum(widths[:k]) for k in range(1, len(widths))], axis=along)
    return tuple((b.reshape(*out.shape[:along], *a.shape[along:]) for a, b in zip(arrays, blocks)))


def joined_along(blocks, dim):
    shape = list(blocks.shape[1:])
    shape[dim] *= blocks.shape[0]
    return jnp.moveaxis(blocks, 0, dim).reshape(shape)


def copy_for_each(array, axis):
    peers = lax.axis_size(axis)
    return lax.all_to_all(
        jnp.broadcast_to(array[None], (peers, *array.shape)), axis, 0, 0, tiled=True
    )


def gather_directly(array, axis, dim):
    return joined_along(copy_for_each(array, axis), dim)


def sent_together(arrays, axis, dim, along):
    widths = [math.prod(a.shape[along:]) for a in arrays]
    both = jnp.concatenate(
        [a.reshape(*a.shape[:along], w) for a, w in zip(arrays, widths)], axis=along
    )
    out = gather_directly(both, axis, dim)
    blocks = jnp.split(out, [sum(widths[:k]) for k in range(1, len(widths))], axis=along)
    return tuple((b.reshape(*out.shape[:along], *a.shape[along:]) for a, b in zip(arrays, blocks)))


def gather_in_order(array, axes, order):
    blocks = array[None]
    for k in order:
        blocks = lax.all_gather(blocks, axes[k], axis=0, tiled=True)
    current = [lax.axis_size(axes[k]) for k in reversed(order)]
    blocks = blocks.reshape(*current, *array.shape)
    turned = sorted(range(len(order)), key=lambda place: order[len(order) - 1 - place])
    return blocks.transpose(*turned, *range(len(order), blocks.ndim)).reshape(-1, *array.shape)


def whole_of(array, axes, order, dim):
    return joined_along(gather_in_order(array, axes, order), dim)


def layer_norm(values):
    centre = values - jnp.mean(values, -1, keepdims=True)
    spread = jnp.mean(centre * centre, -1, keepdims=True)
    return centre * lax.rsqrt(spread + 1e-05)


def perceptron(inputs, w_first, w_second):
    hidden = jax.nn.silu(jnp.dot(inputs, w_first, preferred_element_type=jnp.float32)).astype(
        jnp.bfloat16
    )
    return layer_norm(jnp.dot(hidden, w_second, preferred_element_type=jnp.float32))


def per_device(
    fine_nodes,
    fine_edges,
    fine_senders,
    fine_receivers,
    edge_count,
    ghost_send,
    fine_parent,
    coarse_nodes,
    coarse_edges,
    coarse_senders,
    coarse_receivers,
    edge_in,
    node_in,
    mlp_out,
):
    domains = lax.axis_size(DOM)
    groups = lax.axis_size("grp")
    local = fine_nodes[0]
    node_rows, width = local.shape
    owner_rows = coarse_nodes.shape[0]
    coarse_total = owner_rows * domains
    outgoing = local[ghost_send[0]]
    incoming = lax.all_to_all(outgoing, DOM, split_axis=0, concat_axis=0, tiled=True)
    table = jnp.concatenate([local, incoming.reshape(-1, width)], 0)
    edges = fine_edges[0]
    receivers = fine_receivers[0]
    inputs = jnp.concatenate([edges, local[receivers], table[fine_senders[0]]], -1)
    edge_new = edges.astype(jnp.float32) + perceptron(inputs, edge_in[0], mlp_out[0])
    live = (jnp.arange(edges.shape[0]) < edge_count[0, 0]).astype(jnp.float32)
    summed = jax.ops.segment_sum(
        edge_new * live[:, None], receivers, num_segments=node_rows
    ).astype(jnp.bfloat16)
    fine_mid = (
        local.astype(jnp.float32)
        + perceptron(jnp.concatenate([local, summed], -1), node_in[0], mlp_out[1])
    ).astype(jnp.bfloat16)
    parents = fine_parent[0]
    ones_rows = jnp.ones(parents.shape, jnp.float32)
    mid_wide = fine_mid.astype(jnp.float32)
    piece = owner_rows // groups
    owner = parents // owner_rows
    within = parents % owner_rows
    mapped = within // piece * (domains * piece) + owner * piece + within % piece
    pooled = jax.ops.segment_sum(mid_wide, mapped, num_segments=coarse_total).reshape(
        groups, domains, piece, width
    )
    children = jax.ops.segment_sum(ones_rows, mapped, num_segments=coarse_total).reshape(
        groups, domains, piece
    )
    pooled, children = (
        lax.psum_scatter(
            pooled.astype(jnp.bfloat16), "grp", scatter_dimension=0, tiled=True
        ).astype(jnp.float32),
        lax.psum_scatter(
            children.astype(jnp.bfloat16), "grp", scatter_dimension=0, tiled=True
        ).astype(jnp.float32),
    )
    pooled, children = side_by_side(
        (pooled.astype(jnp.bfloat16), children.astype(jnp.bfloat16)), DOM, 1, 3
    )
    pooled, children = sent_together((pooled, children), "grp", 0, 3)
    pooled = pooled.reshape(owner_rows, width)
    children = children.reshape(owner_rows)
    coarse_mid = ((coarse_nodes.astype(jnp.float32) + pooled) / (1.0 + children)[:, None]).astype(
        jnp.bfloat16
    )
    coarse_table = whole_of(coarse_mid, DOM, (0, 1), 0)
    cinputs = jnp.concatenate(
        [coarse_edges, coarse_mid[coarse_receivers], coarse_table[coarse_senders]], -1
    )
    cedge_new = coarse_edges.astype(jnp.float32) + perceptron(cinputs, edge_in[1], mlp_out[2])
    csummed = jax.ops.segment_sum(cedge_new, coarse_receivers, num_segments=owner_rows).astype(
        jnp.bfloat16
    )
    coarse_out = (
        coarse_mid.astype(jnp.float32)
        + perceptron(jnp.concatenate([coarse_mid, csummed], -1), node_in[1], mlp_out[3])
    ).astype(jnp.bfloat16)
    updated_table = whole_of(coarse_out, DOM, (0, 1), 0)
    above = updated_table[parents]
    fine_out = (
        mid_wide + perceptron(jnp.concatenate([fine_mid, above], -1), node_in[2], mlp_out[4])
    ).astype(jnp.bfloat16)
    return (fine_out[None], coarse_out)


def solution(mesh):
    torus = Mesh(mesh.devices.reshape(mesh.shape["grp"], 4, 8), ("grp", "dom_0", "dom_1"))
    in_specs = (
        P("grp", DOM, None),
        P("grp", DOM, None),
        P("grp", DOM),
        P("grp", DOM),
        P("grp", DOM),
        P("grp", DOM, None),
        P("grp", DOM),
        P(DOM, None),
        P(DOM, None),
        P(DOM),
        P(DOM),
        P(),
        P(),
        P(),
    )
    out_specs = (P("grp", DOM, None), P(DOM, None))
    return jax.shard_map(
        per_device, mesh=torus, in_specs=in_specs, out_specs=out_specs, check_vma=False
    )
```

profile of v0, /device:TPU:1, one launch (start us, length us, event | category | flops | bytes accessed | tf_op | source)
XLA Modules:
  0.0 494.8 jit_solution(16880242438352926247)
XLA Ops:
  8.1 3.2 gather_fusion.1
  11.4 11.9 %all-to-all-start = ((bf16[32,24,128]{2,1,0:T(8,128)(2,1)}), bf16[32,24,128]{2,1,0:T(8,128)(2,1)S(1)}, u32[]{:S(2)}, u32[]{:S(2)}) async-start(bf16[32,24,128]{2,1,0:T(8,128)(2,1)} %bitcast.8), calls=%async_computation | async-start | bytes 393216 | tf_op jit(solution)/shard_map/all_to_all | solution.py:111
  24.0 4.6 scatter_custom_fusion.2
  32.2 27.0 %gather_fusion = bf16[9216,128]{1,0:T(8,128)(2,1)S(1)} fusion(bf16[768,128]{1,0:T(8,128)(2,1)S(1)} %bitcast.111, s32[9216]{0:T(1024)S(1)} %broadcast_clamp_fusion.1), kind=kCustom, calls=%fused_computation | custom fusion | bytes 4755456 | tf_op jit(solution)/shard_map/gather | solution.py:115
  59.2 2.5 copy.87
  61.7 4.3 copy.81
  67.1 27.0 %gather_fusion.2 = bf16[9216,128]{1,0:T(8,128)(2,1)S(1)} fusion(bf16[1536,128]{1,0:T(8,128)(2,1)S(1)} %copy.86, s32[9216]{0:T(1024)S(1)} %broadcast_clamp_fusion), kind=kCustom, calls=%fused_computation.2 | custom fusion | bytes 4755456 | tf_op jit(solution)/shard_map/gather | solution.py:115
  94.1 2.5 copy.88
  96.7 6.8 %fusion.114 = (f32[9216]{0:T(1024)S(1)}, f32[9216,128]{0,1:T(8,128)}) fusion(bf16[5,128,128]{2,1,0:T(8,128)(2,1)} %param.27, bf16[9216,128]{0,1:T(8,128)(2,1)} %copy.88, bf16[9216,128]{0,1:T(8,128)(2,1)} %copy.87, bf16[9216,128]{0,1:T(8,128)(2,1)} %bitcast.114, bf16[2,384,128]{2,1,0:T(8,128)(2,1)S(1)} %copy-done.7), kind=kOutput, calls=%fused_computation.141 | convolution fusion | flops 1236261888 | bytes 11964416 | tf_op jit(solution)/shard_map/dot_general | solution.py:85
  103.4 3.0 multiply_reduce_fusion
  107.2 3.0 add_multiply_fusion
  110.2 6.1 %copy.89 = f32[9216,128]{1,0:T(8,128)} copy(f32[9216,128]{0,1:T(8,128)} %add_multiply_fusion) | data formatting | bytes 9437184 | tf_op jit(solution)/shard_map/mul | solution.py:119
  116.3 61.0 %scatter_custom_fusion = f32[768,128]{1,0:T(8,128)S(1)} fusion(s32[9216]{0:T(1024)} %bitcast.128, f32[9216,128]{1,0:T(8,128)} %copy.89, f32[]{:T(128)} %constant.85.clone.1), kind=kCustom, calls=%fused_computation.68 | custom fusion | flops 1179648 | bytes 393728 | tf_op jit(solution)/shard_map/scatter-add | solution.py:118
  179.1 9.7 %scatter_custom_fusion.1 = f32[16384,128]{1,0:T(8,128)} fusion(s32[768]{0:T(1024)S(1)} %get-tuple-element.11, f32[768,128]{1,0:T(8,128)S(1)} %copy.92, f32[]{:T(128)} %constant.85.clone.1), kind=kCustom, calls=%fused_computation.19 | custom fusion | flops 98304 | bytes 8388612 | tf_op jit(solution)/shard_map/scatter-add | solution.py:132
  188.8 5.1 %convert_element_type.86 = bf16[16384,128]{1,0:T(8,128)(2,1)} convert(f32[16384,128]{1,0:T(8,128)} %scatter_custom_fusion.1) | non-fusion elementwise | flops 2097152 | bytes 12582912 | tf_op jit(solution)/shard_map/convert_element_type | solution.py:140
  195.0 38.5 %reduce-scatter.3.cloned.1.call-done = bf16[1,32,64,128]{3,2,1,0:T(8,128)(2,1)} async-done(((bf16[8,32,64,128]{3,2,1,0:T(8,128)(2,1)}), bf16[1,32,64,128]{3,2,1,0:T(8,128)(2,1)}) %reduce-scatter.3.cloned.1.call-update) | async-done | bytes 524304 | tf_op jit(solution)/shard_map/reduce_scatter | solution.py:139
  234.8 30.8 %all_to_all.15 = bf16[32,1,1,64,129]{4,3,2,1,0:T(8,128)(2,1)S(1)} all-to-all(bf16[32,1,1,64,129]{4,3,2,1,0:T(8,128)(2,1)S(1)} %maximum_bitcast_fusion), channel_id=1, replica_groups=mesh['grp'=8,'dom_0'=4,'dom_1'=8] {'dom_0','dom_1'}, dimensions={0} | all-to-all | bytes 1056768 | tf_op jit(solution)/shard_map/all_to_all | solution.py:20
  266.7 12.0 %all-to-all-start.2 = ((f32[8,1,1,64,129]{4,3,2,1,0:T(8,128)}), f32[8,1,1,64,129]{4,3,2,1,0:T(8,128)S(1)}, u32[]{:S(2)}, u32[]{:S(2)}) async-start(f32[8,1,1,64,129]{4,3,2,1,0:T(8,128)} %broadcast_in_dim.28), calls=%async_computation.4 | async-start | bytes 1048576 | tf_op jit(solution)/shard_map/all_to_all | solution.py:42
  278.9 9.2 %all-to-all-done.2 = f32[8,1,1,64,129]{4,3,2,1,0:T(8,128)S(1)} async-done(((f32[8,1,1,64,129]{4,3,2,1,0:T(8,128)}), f32[8,1,1,64,129]{4,3,2,1,0:T(8,128)S(1)}, u32[]{:S(2)}, u32[]{:S(2)}) %all-to-all-start.2) | async-done | bytes 264224 | tf_op jit(solution)/shard_map/all_to_all | solution.py:42
  288.5 9.9 %all-gather = bf16[2048,128]{0,1:T(8,128)(2,1)S(1)} all-gather(bf16[512,128]{0,1:T(8,128)(2,1)S(1)} %divide_convert_fusion), channel_id=2, replica_groups=mesh['grp'=8,'dom_0'=4,'dom_1'=8] {'dom_0'}, dimensions={0}, use_global_device_ids=true | all-gather | bytes 655360 | tf_op jit(solution)/shard_map/all_gather | solution.py:64
  300.4 14.9 %gather_fusion.3 = bf16[4096,128]{1,0:T(8,128)(2,1)} fusion(bf16[512,128]{1,0:T(8,128)(2,1)S(1)} %copy.96, s32[4096]{0:T(1024)S(1)} %fusion.94), kind=kCustom, calls=%fused_computation.3 | custom fusion | bytes 2113536 | tf_op jit(solution)/shard_map/gather | solution.py:157
  315.3 37.2 %all-gather.5.cloned.1.call-done = bf16[32,512,128]{2,1,0:T(8,128)(2,1)} async-done(((bf16[4,512,128]{2,1,0:T(8,128)(2,1)}), bf16[32,512,128]{2,1,0:T(8,128)(2,1)}) %all-gather.5.cloned.1.call-update) | async-done | bytes 4194320 | tf_op jit(solution)/shard_map/all_gather | solution.py:64
  352.5 4.6 copy.98
  357.1 16.9 %gather_fusion.4 = bf16[4096,128]{1,0:T(8,128)(2,1)} fusion(bf16[16384,128]{1,0:T(8,128)(2,1)} %bitcast.112, s32[4096]{0:T(1024)S(1)} %fusion.95), kind=kCustom, calls=%fused_computation.4 | custom fusion | bytes 2113536 | tf_op jit(solution)/shard_map/gather | solution.py:157
  374.1 3.3 fusion.124
  377.7 1.7 multiply_add_fusion
  379.3 1.9 copy.99
  381.3 26.5 %scatter_custom_fusion.3 = f32[512,128]{1,0:T(8,128)S(1)} fusion(s32[4096]{0:T(1024)S(1)} %copy-done.6, f32[4096,128]{1,0:T(8,128)S(1)} %copy.99, f32[]{:T(128)} %constant.85.clone.1), kind=kCustom, calls=%fused_computation.71 | custom fusion | flops 524288 | bytes 262148 | tf_op jit(solution)/shard_map/scatter-add | solution.py:160
  409.2 11.6 %all-gather.1 = bf16[2048,128]{0,1:T(8,128)(2,1)S(1)} all-gather(bf16[512,128]{0,1:T(8,128)(2,1)S(1)} %add_convert_fusion.2), channel_id=3, replica_groups=mesh['grp'=8,'dom_0'=4,'dom_1'=8] {'dom_0'}, dimensions={0}, use_global_device_ids=true | all-gather | bytes 655360 | tf_op jit(solution)/shard_map/all_gather | solution.py:64
  422.7 54.3 %all-gather.7.cloned.1.call-done = bf16[32,512,128]{2,1,0:T(8,128)(2,1)} async-done(((bf16[4,512,128]{2,1,0:T(8,128)(2,1)}), bf16[32,512,128]{2,1,0:T(8,128)(2,1)}) %all-gather.7.cloned.1.call-update) | async-done | bytes 4194320 | tf_op jit(solution)/shard_map/all_gather | solution.py:64
  477.0 4.6 copy.102
  481.6 4.3 gather_fusion.5
  (88 shorter events, 19.8 us)
Async XLA Ops:
  7.2 25.0 %copy-start = (bf16[1,768,128]{2,1,0:T(8,128)(2,1)S(1)}, bf16[1,768,128]{2,1,0:T(8,128)(2,1)}, u32[]{:S(2)}) copy-start(bf16[1,768,128]{2,1,0:T(8,128)(2,1)} %param.14) | copy-start | bytes 589828
  11.4 55.3 %all-to-all-start = ((bf16[32,24,128]{2,1,0:T(8,128)(2,1)}), bf16[32,24,128]{2,1,0:T(8,128)(2,1)S(1)}, u32[]{:S(2)}, u32[]{:S(2)}) async-start(bf16[32,24,128]{2,1,0:T(8,128)(2,1)} %bitcast.8), calls=%async_computation | async-start | bytes 393216 | tf_op jit(solution)/shard_map/all_to_all | solution.py:111
  23.2 170.7 %reduce-scatter.5.cloned.1.call-start = ((), (), s32[]{:S(2)}) async-start(), calls=%async_computation.6 | async-start | bytes 73728 | tf_op jit(solution)/shard_map/reduce_scatter | solution.py:142
  29.4 204.1 %reduce-scatter.3.cloned.1.call-start = ((), (), s32[]{:S(2)}) async-start(), calls=%async_computation.5 | async-start | bytes 4718592 | tf_op jit(solution)/shard_map/reduce_scatter | solution.py:139
  94.1 2.5 copy-start.7
  96.7 9.8 %copy-start.2 = (bf16[1,9216,128]{1,2,0:T(8,128)(2,1)S(1)}, bf16[1,9216,128]{1,2,0:T(8,128)(2,1)}, u32[]{:S(2)}) copy-start(bf16[1,9216,128]{1,2,0:T(8,128)(2,1)} %copy.81) | copy-start | bytes 7077892
  103.4 3.8 copy-start.1
  195.0 83.7 %copy-start.4 = (bf16[512,128]{1,0:T(8,128)(2,1)S(1)}, bf16[512,128]{1,0:T(8,128)(2,1)}, u32[]{:S(2)}) copy-start(bf16[512,128]{1,0:T(8,128)(2,1)} %param.21) | copy-start | bytes 393220
  265.8 33.8 %copy-start.3 = (bf16[4096,128]{1,0:T(8,128)(2,1)S(1)}, bf16[4096,128]{1,0:T(8,128)(2,1)}, u32[]{:S(2)}) copy-start(bf16[4096,128]{1,0:T(8,128)(2,1)} %param.22) | copy-start | bytes 3145732
  266.7 21.4 %all-to-all-start.2 = ((f32[8,1,1,64,129]{4,3,2,1,0:T(8,128)}), f32[8,1,1,64,129]{4,3,2,1,0:T(8,128)S(1)}, u32[]{:S(2)}, u32[]{:S(2)}) async-start(f32[8,1,1,64,129]{4,3,2,1,0:T(8,128)} %broadcast_in_dim.28), calls=%async_computation.4 | async-start | bytes 1048576 | tf_op jit(solution)/shard_map/all_to_all | solution.py:42
  278.7 73.8 %all-gather.5.cloned.1.call-start = ((), (), s32[]{:S(2)}) async-start(), calls=%async_computation.7 | async-start | bytes 4718592 | tf_op jit(solution)/shard_map/all_gather | solution.py:64
  278.8 21.4 %copy-start.5 = (s32[4096]{0:T(1024)S(1)}, s32[4096]{0:T(1024)}, u32[]{:S(2)}) copy-start(s32[4096]{0:T(1024)} %param.23) | copy-start | bytes 49156
  278.8 21.4 %copy-start.6 = (s32[4096]{0:T(1024)S(1)}, s32[4096]{0:T(1024)}, u32[]{:S(2)}) copy-start(s32[4096]{0:T(1024)} %param.24) | copy-start | bytes 49156
  299.4 177.6 %all-gather.7.cloned.1.call-start = ((), (), s32[]{:S(2)}) async-start(), calls=%async_computation.8 | async-start | bytes 4718592 | tf_op jit(solution)/shard_map/all_gather | solution.py:64
  379.3 28.6 %copy-start.8 = (bf16[3,256,128]{2,1,0:T(8,128)(2,1)S(1)}, bf16[3,256,128]{2,1,0:T(8,128)(2,1)}, u32[]{:S(2)}) copy-start(bf16[3,256,128]{2,1,0:T(8,128)(2,1)} %param.26) | copy-start | bytes 589828
Sparse Core Ops, SparseCore 0:
  29.5 32.7 reduce-scatter.4
  194.0 39.4 reduce-scatter.2
  299.5 52.9 all-gather.4
  422.0 54.8 all-gather.6
where the time goes:
time: 496 us; the launch traced here: 495 us
  waiting for transfers between devices  139 us (28%)
  local copies, waits for them, and re-layouts  130 us (26%)
  other arithmetic  120 us (24%)
  blocking collectives  52.4 us (11%)
  starting transfers between devices  24.2 us (5%)
  between operations  14.9 us (3%)
  matrix products  14 us (3%)
    all_gather x2, waiting for transfers between devices, gather_in_order(): blocks = lax.all_gather(blocks, axes[k], axis=0, tiled=True)  91.5 us
    scatter-add x1, other arithmetic, per_device(): jax.ops.segment_sum(edge_new * live[:, None], receivers, num_segments=nod...  61 us
    reduce_scatter x1, waiting for transfers between devices, per_device(): lax.psum_scatter(pooled.astype(jnp.bfloat16), 'grp', scatter_dimension=0,...  38.5 us
    all_to_all x1, blocking collectives, summed_on_arrival(): lax.all_to_all(in_blocks(array, dim, peers), axis, 0, 0, tiled=True)  30.8 us
    gather x2, local copies, waits for them, and re-layouts, per_device(): local[receivers]  29.5 us
    gather x2, local copies, waits for them, and re-layouts, per_device(): table[fine_senders[0]]  29.5 us
    scatter-add x1, other arithmetic, per_device(): jax.ops.segment_sum(cedge_new, coarse_receivers, num_segments=owner_rows)  26.5 us
    all_gather x2, blocking collectives, gather_in_order(): blocks = lax.all_gather(blocks, axes[k], axis=0, tiled=True)  21.5 us
  transfers between devices with their start and end apart: 6, of which 4 were waited for; matrix products, arithmetic and copies ran while one was open for 38% of the time, Pallas kernels for 0%

commit v1 on v0

v1 whole, which is shorter than its diff:
```python
import functools

import jax
import jax.numpy as jnp
from jax import lax
from jax.experimental import pallas as pl
from jax.experimental.pallas import tpu as pltpu
from jax.sharding import PartitionSpec as P

BF = jnp.bfloat16
F32 = jnp.float32
I32 = jnp.int32
POOL = 24
POOL_PAD = 32
ASK = 48
ASK_PAD = 64
NT = (((1,), (1,)), ((), ()))


def dot(a, b):
    return jnp.dot(a, b, preferred_element_type=F32)


def iota(shape, axis):
    return lax.broadcasted_iota(I32, shape, axis)


def as_bf(mask):
    return jnp.where(mask, 1.0, 0.0).astype(BF)


def column(row):
    n = row.shape[1]
    return jnp.concatenate(
        [jnp.broadcast_to(row[:, k : k + 128], (128, 128)).T for k in range(0, n, 128)], 0
    )


def pick_rows(col, width):
    n = col.shape[0]
    lane = iota((n, 128), 1)
    return jnp.concatenate([as_bf(col == lane + k) for k in range(0, width, 128)], 1)


def pick_into(row, height, first=0):
    return as_bf(iota((height, row.shape[1]), 0) + first == row)


def mean_of(w):
    mean = jnp.mean(w.astype(F32), axis=1, keepdims=True)
    return jnp.concatenate([w, jnp.broadcast_to(mean, w.shape).astype(BF)], axis=1)


def averager():
    return jnp.full((128, 128), 1.0 / 128, BF)


def second(x, w_mean, ones):
    hidden = (x / (1.0 + jnp.exp(-x))).astype(BF)
    y = dot(hidden, w_mean)
    centre = y[:, :128] - y[:, 128:]
    spread = dot((centre * centre).astype(BF), ones)
    return centre * lax.rsqrt(spread + 1e-5)


def vmem(n):
    return [pl.BlockSpec(memory_space=pltpu.VMEM)] * n


def fine_kernel(
    block, count, edges_ref, snd_ref, rcv_ref, local_ref, ghost_ref, ein_ref, nin_ref, out_w, out_ref,
    by_sender, by_receiver, total, w_mean,
):
    step = pl.program_id(0)
    nodes = local_ref.shape[0]
    half = nodes // 2
    ones = averager()

    @pl.when(step == 0)
    def _():
        local = local_ref[...]
        by_sender[:, :128] = dot(local, ein_ref[0, 256:384, :]).astype(BF)
        by_sender[:, 128:] = dot(ghost_ref[...], ein_ref[0, 256:384, :]).astype(BF)
        mine = dot(local, ein_ref[0, 128:256, :]).astype(BF)
        by_receiver[:, :128] = mine[:half]
        by_receiver[:, 128:] = mine[half:]
        total[...] = jnp.zeros_like(total)
        w_mean[0] = mean_of(out_w[0])
        w_mean[1] = mean_of(out_w[1])

    receivers = rcv_ref[0]
    scol = column(snd_ref[0])
    rcol = column(receivers)
    s_upper = scol >= nodes
    r_upper = rcol >= half
    from_s = dot(pick_rows(jnp.where(s_upper, scol - nodes, scol), nodes), by_sender[...])
    from_r = dot(pick_rows(jnp.where(r_upper, rcol - half, rcol), half), by_receiver[...])
    edge = edges_ref[...]
    x = (
        dot(edge, ein_ref[0, 0:128, :])
        + jnp.where(s_upper, from_s[:, 128:], from_s[:, :128])
        + jnp.where(r_upper, from_r[:, 128:], from_r[:, :128])
    )
    new = edge.astype(F32) + second(x, w_mean[0], ones)
    sides = jnp.concatenate([jnp.where(r_upper, 0.0, new), jnp.where(r_upper, new, 0.0)], 1)
    slot = step * block + iota((1, block), 1)
    into = jnp.where(receivers >= half, receivers - half, receivers)
    into = jnp.where(slot < count[0, 0], into, -1)
    total[...] += dot(pick_into(into, half), sides.astype(BF))

    @pl.when(step == pl.num_programs(0) - 1)
    def _():
        agg = jnp.concatenate([total[:, :128], total[:, 128:]], 0).astype(BF)
        local = local_ref[...]
        x = dot(local, nin_ref[0, 0:128, :]) + dot(agg, nin_ref[0, 128:256, :])
        out_ref[...] = (local.astype(F32) + second(x, w_mean[1], ones)).astype(BF)


def fine_step(count, edges, senders, receivers, local, ghost, edge_in, node_in, mlp_out, block=1024):
    slots, nodes = edges.shape[0], local.shape[0]
    steps = slots // block
    whole = lambda a: pl.BlockSpec(a.shape, lambda i: (0,) * a.ndim)
    index = pl.BlockSpec((1, 1, block), lambda i: (i, 0, 0))
    return pl.pallas_call(
        functools.partial(fine_kernel, block),
        grid=(steps,),
        name="fine_edges",
        out_shape=jax.ShapeDtypeStruct((nodes, 128), BF),
        in_specs=[
            pl.BlockSpec(memory_space=pltpu.SMEM), pl.BlockSpec((block, 128), lambda i: (i, 0)), index, index,
            whole(local), whole(ghost), whole(edge_in), whole(node_in), whole(mlp_out),
        ],
        out_specs=pl.BlockSpec((nodes, 128), lambda i: (0, 0)),
        scratch_shapes=[
            pltpu.VMEM((nodes, 256), BF), pltpu.VMEM((nodes // 2, 256), BF), pltpu.VMEM((nodes // 2, 256), F32),
            pltpu.VMEM((2, 128, 256), BF),
        ],
    )(
        count, edges, senders.reshape(steps, 1, block), receivers.reshape(steps, 1, block),
        local, ghost, edge_in, node_in, mlp_out,
    )


def each_peer(axis, body):
    me, peers = lax.axis_index(axis), lax.axis_size(axis)

    def one(step, carry):
        body(lax.rem(me + step, peers))
        return carry

    lax.fori_loop(1, peers, one, 0)


def greet(axes):
    barrier = pltpu.get_barrier_semaphore()
    for axis in axes:
        each_peer(axis, lambda peer, axis=axis: pl.semaphore_signal(barrier, inc=1, device_id={axis: peer}))


def all_here(axes):
    pl.semaphore_wait(pltpu.get_barrier_semaphore(), sum(lax.axis_size(axis) - 1 for axis in axes))


def send(axis, source, target, sems):
    me = lax.axis_index(axis)

    def one(peer):
        pltpu.make_async_remote_copy(
            src_ref=source(peer), dst_ref=target(me), send_sem=sems.at[0], recv_sem=sems.at[1],
            device_id={axis: peer},
        ).start()

    each_peer(axis, one)


def arrived(axis, span, sems):
    peer = lax.rem(lax.axis_index(axis) + 1, lax.axis_size(axis))
    whole = pltpu.make_async_remote_copy(
        src_ref=span, dst_ref=span, send_sem=sems.at[0], recv_sem=sems.at[1], device_id={axis: peer}
    )
    whole.wait()


def ranked(owner, owners):
    n = owner.shape[1]
    theirs = iota((owners, n), 0) == owner
    before = as_bf(iota((n, n), 0) < iota((n, n), 1))
    counts = dot(as_bf(theirs), before)
    return jnp.sum(jnp.where(theirs, counts, 0.0), axis=0, keepdims=True).astype(I32), theirs


def listed(theirs, value, lane):
    n = value.shape[1]
    code = value + 1
    low, high = (code & 255).astype(F32), (code >> 8).astype(F32)
    parts = jnp.concatenate([jnp.where(theirs, low, 0.0), jnp.where(theirs, high, 0.0)], 0)
    there = as_bf(iota((128, n), 0) == lane)
    out = lax.dot_general(parts.astype(BF), there, NT, preferred_element_type=F32)
    owners = theirs.shape[0]
    return (out[:owners] + 256.0 * out[owners:]).astype(I32)


def early_kernel(
    local_ref, ghost_ids, parents, csenders, ghost_out, place_out, cplace_out, pool_out, ask_out, flag_out,
    ghost_tx, ghost_rx, note_tx, note_rx, flag_rx, flag_tx, ghost_sems, note_sems, flag_sems,
):
    me, grp = lax.axis_index("dom"), lax.axis_index("grp")
    peers, groups = lax.axis_size("dom"), lax.axis_size("grp")
    shift = 9
    rows = ghost_tx.shape[1]
    greet(("dom", "grp"))
    picks = dot(pick_rows(column(ghost_ids[...]), local_ref.shape[0]), local_ref[...])
    for p in range(peers):
        ghost_tx[p] = picks[p * rows : (p + 1) * rows].astype(BF)

    all_here(("dom", "grp"))
    send("dom", lambda peer: ghost_tx.at[peer], lambda me: ghost_rx.at[me], ghost_sems)
    ghost_rx[me] = ghost_tx[me]

    parent = parents[...]
    owner, within = parent >> shift, parent & ((1 << shift) - 1)
    rank, theirs = ranked(owner, peers)
    away = owner != me
    place_out[...] = jnp.where(away, (1 << shift) + owner * POOL_PAD + rank, within)
    excess = jnp.max(jnp.where(away & (rank >= POOL), 1, 0), axis=1, keepdims=True)
    pool_note = listed(theirs, within, rank + lax.rem(me, 4) * POOL_PAD)

    sender = csenders[grp]
    owner, within = sender >> shift, sender & ((1 << shift) - 1)
    rank, theirs = ranked(owner, peers)
    away = owner != me
    cplace_out[...] = jnp.where(away, (1 << shift) + owner * ASK_PAD + rank, within)
    excess = jnp.maximum(excess, jnp.max(jnp.where(away & (rank >= ASK), 1, 0), axis=1, keepdims=True))
    ask_note = listed(theirs, within, rank + lax.rem(me, 2) * ASK_PAD)

    flag_tx[...] = jnp.broadcast_to(excess, (1, 128))
    send("grp", lambda peer: flag_tx, lambda grp: flag_rx.at[grp], flag_sems)
    flag_rx[grp] = flag_tx[...]
    for p in range(peers):
        note_tx[p, :, 0:128] = pool_note[p : p + 1]
        note_tx[p, :, 128:256] = ask_note[p : p + 1]
    arrived("grp", flag_rx.at[pl.ds(0, groups - 1)], flag_sems)
    flag = flag_rx[0]
    for k in range(1, groups):
        flag = jnp.maximum(flag, flag_rx[k])
    for p in range(peers):
        note_tx[p, :, 256:384] = flag
    send("dom", lambda peer: note_tx.at[peer], lambda me: note_rx.at[me], note_sems)
    note_rx[me] = jnp.concatenate([jnp.zeros((1, 256), I32), flag], 1)
    arrived("dom", note_rx.at[pl.ds(0, peers - 1)], note_sems)
    notes = [note_rx[p] for p in range(peers)]
    for k in range(0, peers, 4):
        pool_out[k // 4 : k // 4 + 1, :] = sum(n[:, 0:128] for n in notes[k : k + 4])
    for k in range(0, peers, 2):
        ask_out[k // 2 : k // 2 + 1, :] = sum(n[:, 128:256] for n in notes[k : k + 2])
    for n in notes:
        flag = jnp.maximum(flag, n[:, 256:384])
    flag_out[...] = flag
    arrived("dom", ghost_rx.at[pl.ds(0, peers - 1)], ghost_sems)
    ghost_out[...] = ghost_rx[...]


def early_step(local, ghost_send, parents, csenders, groups):
    peers, rows = ghost_send.shape
    edges = csenders.shape[0] // groups
    return pl.pallas_call(
        early_kernel,
        name="early",
        out_shape=[
            jax.ShapeDtypeStruct((peers, rows, 128), BF),
            jax.ShapeDtypeStruct((1, parents.shape[0]), I32),
            jax.ShapeDtypeStruct((1, edges), I32),
            jax.ShapeDtypeStruct((peers // 4, 128), I32),
            jax.ShapeDtypeStruct((peers // 2, 128), I32),
            jax.ShapeDtypeStruct((1, 128), I32),
        ],
        in_specs=vmem(4),
        out_specs=vmem(6),
        scratch_shapes=[
            pltpu.VMEM((peers, rows, 128), BF), pltpu.VMEM((peers, rows, 128), BF),
            pltpu.VMEM((peers, 1, 384), I32), pltpu.VMEM((peers, 1, 384), I32),
            pltpu.VMEM((groups, 1, 128), I32), pltpu.VMEM((1, 128), I32),
            pltpu.SemaphoreType.DMA((2,)), pltpu.SemaphoreType.DMA((2,)), pltpu.SemaphoreType.DMA((2,)),
        ],
        compiler_params=pltpu.CompilerParams(collective_id=0, has_side_effects=True),
    )(local, ghost_send.reshape(1, -1), parents.reshape(1, -1), csenders.reshape(groups, 1, edges))


def late_kernel(
    mid_ref, place_ref, cplace_ref, pool_ref, ask_ref, cnodes_ref, cedges_hbm, crecv_ref, ein_ref, nin_ref, out_w,
    fine_out, coarse_out,
    cedges, up_tx, up_rx, count_tx, count_rx, part_tx, part_rx, cmid, ask_tx, ask_rx, cpart_tx, cpart_rx, cout,
    down_tx, down_rx, ask_sel, down_sel, csel, fsel, edge_sem, sems,
):
    me, grp = lax.axis_index("dom"), lax.axis_index("grp")
    peers, groups = lax.axis_size("dom"), lax.axis_size("grp")
    others, friends = peers - 1, groups - 1
    own = cnodes_ref.shape[0]
    piece = own // groups
    nedges = cedges.shape[0]
    ones = averager()
    ups, asks = peers * POOL_PAD, peers * ASK_PAD
    fetch = pltpu.make_async_copy(
        cedges_hbm.at[pl.ds(pl.multiple_of(grp * nedges, nedges), nedges)], cedges, edge_sem
    )
    fetch.start()
    up_rx[...] = jnp.zeros_like(up_rx)
    down_rx[...] = jnp.zeros_like(down_rx)
    ask_rx[...] = jnp.zeros_like(ask_rx)
    greet(("dom", "grp"))

    mid, place = mid_ref[...], place_ref[...]
    up_tx[...] = dot(pick_into(place, ups, own), mid).astype(BF).reshape(up_tx.shape)
    all_here(("dom", "grp"))
    few, some = pl.ds(0, POOL), pl.ds(0, ASK)
    send("dom", lambda p: up_tx.at[p, few], lambda m: up_rx.at[m, few], sems.at[0])

    here = pick_into(place, own)
    pool_rows = jnp.concatenate([pool_ref[k : k + 1, :] for k in range(pool_ref.shape[0])], 1) - 1
    there = pick_into(pool_rows, own)
    counts = lax.dot_general(jnp.full((8, here.shape[1]), 1.0, BF), here, NT, preferred_element_type=F32)
    counts += lax.dot_general(jnp.full((8, ups), 1.0, BF), there, NT, preferred_element_type=F32)
    count_tx[...] = counts[0:1]
    send("grp", lambda p: count_tx, lambda m: count_rx.at[m], sems.at[1])
    count_rx[grp] = count_tx[...]
    pooled = dot(here, mid)
    for k in range(ask_ref.shape[0]):
        ask_sel[128 * k : 128 * (k + 1), :] = pick_rows(column(ask_ref[k : k + 1, :] - 1), own)
    for k in range(pool_ref.shape[0]):
        down_sel[128 * k : 128 * (k + 1), :] = pick_rows(column(pool_ref[k : k + 1, :] - 1), own)
    csel[...] = pick_rows(column(cplace_ref[...]), own + asks)
    fsel[...] = pick_rows(column(place), own + ups)
    receivers = crecv_ref[grp]
    into = pick_into(receivers, own)
    from_r = pick_rows(column(receivers), own)
    w_edge, w_node, w_back = mean_of(out_w[2]), mean_of(out_w[3]), mean_of(out_w[4])
    arrived("grp", count_rx.at[pl.ds(0, friends)], sems.at[1])
    children = count_rx[0]
    for k in range(1, groups):
        children = children + count_rx[k]
    diagonal = iota((piece, own), 1) == iota((piece, own), 0) + grp * piece
    children = jnp.sum(jnp.where(diagonal, children, 0.0), axis=1, keepdims=True)

    arrived("dom", up_rx.at[pl.ds(0, others), few], sems.at[0])
    pooled += dot(there, up_rx[...].reshape(ups, 128))
    part_tx[...] = pooled.astype(BF).reshape(part_tx.shape)
    send("grp", lambda p: part_tx.at[p], lambda m: part_rx.at[m], sems.at[2])
    part_rx[grp] = part_tx[grp]
    arrived("grp", part_rx.at[pl.ds(0, friends)], sems.at[2])
    mine = pl.ds(pl.multiple_of(grp * piece, piece), piece)
    sums = cnodes_ref[mine, :].astype(F32)
    for k in range(groups):
        sums = sums + part_rx[k].astype(F32)
    own_mid = (sums / (1.0 + children)).astype(BF)
    cmid[grp] = own_mid
    send("grp", lambda p: cmid.at[grp], lambda m: cmid.at[m], sems.at[3])
    arrived("grp", cmid.at[pl.ds(0, friends)], sems.at[3])

    coarse = cmid[...].reshape(own, 128)
    ask_tx[...] = dot(ask_sel[...], coarse).astype(BF).reshape(ask_tx.shape)
    send("dom", lambda p: ask_tx.at[p, some], lambda m: ask_rx.at[m, some], sems.at[4])
    fetch.wait()
    edge = cedges[...]
    x = dot(edge, ein_ref[1, 0:128, :]) + dot(dot(from_r, coarse).astype(BF), ein_ref[1, 128:256, :])
    sender = dot(csel[:, 0:own], coarse)
    arrived("dom", ask_rx.at[pl.ds(0, others), some], sems.at[4])
    sender += dot(csel[:, own:], ask_rx[...].reshape(asks, 128))
    x += dot(sender.astype(BF), ein_ref[1, 256:384, :])
    new = edge.astype(F32) + second(x, w_edge, ones)
    cpart_tx[...] = dot(into, new.astype(BF)).astype(BF).reshape(cpart_tx.shape)
    send("grp", lambda p: cpart_tx.at[p], lambda m: cpart_rx.at[m], sems.at[5])
    cpart_rx[grp] = cpart_tx[grp]
    x = dot(own_mid, nin_ref[1, 0:128, :])
    arrived("grp", cpart_rx.at[pl.ds(0, friends)], sems.at[5])
    sums = cpart_rx[0].astype(F32)
    for k in range(1, groups):
        sums = sums + cpart_rx[k].astype(F32)
    x += dot(sums.astype(BF), nin_ref[1, 128:256, :])
    cout[grp] = (own_mid.astype(F32) + second(x, w_node, ones)).astype(BF)
    send("grp", lambda p: cout.at[grp], lambda m: cout.at[m], sems.at[6])
    arrived("grp", cout.at[pl.ds(0, friends)], sems.at[6])

    coarse = cout[...].reshape(own, 128)
    down_tx[...] = dot(down_sel[...], coarse).astype(BF).reshape(down_tx.shape)
    send("dom", lambda p: down_tx.at[p, few], lambda m: down_rx.at[m, few], sems.at[7])
    coarse_out[...] = coarse
    above = dot(fsel[:, 0:own], coarse)
    x = dot(mid, nin_ref[2, 0:128, :])
    arrived("dom", down_rx.at[pl.ds(0, others), few], sems.at[7])
    above += dot(fsel[:, own:], down_rx[...].reshape(ups, 128))
    x += dot(above.astype(BF), nin_ref[2, 128:256, :])
    fine_out[...] = (mid.astype(F32) + second(x, w_back, ones)).astype(BF)


def late_step(
    mid, place, cplace, pool, ask, coarse_nodes, coarse_edges, coarse_receivers, edge_in, node_in, mlp_out
):
    peers, groups = lax.axis_size("dom"), lax.axis_size("grp")
    own, nodes = coarse_nodes.shape[0], mid.shape[0]
    edges, piece = coarse_edges.shape[0] // groups, own // groups
    pieces = lambda: pltpu.VMEM((groups, piece, 128), BF)
    specs = vmem(6) + [pl.BlockSpec(memory_space=pl.ANY)] + vmem(4)
    return pl.pallas_call(
        late_kernel,
        name="late",
        out_shape=[jax.ShapeDtypeStruct((nodes, 128), BF), jax.ShapeDtypeStruct((own, 128), BF)],
        in_specs=specs,
        out_specs=vmem(2),
        scratch_shapes=[
            pltpu.VMEM((edges, 128), BF),
            pltpu.VMEM((peers, POOL_PAD, 128), BF), pltpu.VMEM((peers, POOL_PAD, 128), BF),
            pltpu.VMEM((1, own), F32), pltpu.VMEM((groups, 1, own), F32),
            pieces(), pieces(), pieces(),
            pltpu.VMEM((peers, ASK_PAD, 128), BF), pltpu.VMEM((peers, ASK_PAD, 128), BF),
            pieces(), pieces(), pieces(),
            pltpu.VMEM((peers, POOL_PAD, 128), BF), pltpu.VMEM((peers, POOL_PAD, 128), BF),
            pltpu.VMEM((peers * ASK_PAD, own), BF), pltpu.VMEM((peers * POOL_PAD, own), BF),
            pltpu.VMEM((edges, own + peers * ASK_PAD), BF), pltpu.VMEM((nodes, own + peers * POOL_PAD), BF),
            pltpu.SemaphoreType.DMA, pltpu.SemaphoreType.DMA((8, 2)),
        ],
        compiler_params=pltpu.CompilerParams(collective_id=1, has_side_effects=True),
    )(
        mid, place, cplace, pool, ask, coarse_nodes, coarse_edges, coarse_receivers.reshape(groups, 1, edges),
        edge_in, node_in, mlp_out,
    )


def layer_norm(values):
    centre = values - jnp.mean(values, -1, keepdims=True)
    spread = jnp.mean(centre * centre, -1, keepdims=True)
    return centre * lax.rsqrt(spread + 1e-05)


def perceptron(inputs, w_first, w_second):
    hidden = jax.nn.silu(jnp.dot(inputs, w_first, preferred_element_type=F32)).astype(BF)
    return layer_norm(jnp.dot(hidden, w_second, preferred_element_type=F32))


def summed(array, axis):
    return jnp.sum(lax.all_to_all(array, axis, 0, 0, tiled=True), axis=0)


def all_of(array, axis):
    peers = lax.axis_size(axis)
    copies = lax.all_to_all(jnp.broadcast_to(array[None], (peers, *array.shape)), axis, 0, 0, tiled=True)
    return copies.reshape(peers * array.shape[0], *array.shape[1:])


def dense_step(
    mid, parents, coarse_nodes, coarse_edges, coarse_senders, coarse_receivers, edge_in, node_in, mlp_out
):
    peers, groups = lax.axis_size("dom"), lax.axis_size("grp")
    own = coarse_nodes.shape[0]
    piece = own // groups
    wide = jnp.concatenate([mid.astype(F32), jnp.ones(mid.shape, F32)], -1)
    sums = jax.ops.segment_sum(wide, parents, num_segments=own * peers)
    sums = jnp.moveaxis(sums.reshape(peers, groups, piece, 256), 1, 0)
    sums = all_of(summed(summed(sums, "grp"), "dom"), "grp")
    coarse_mid = ((coarse_nodes.astype(F32) + sums[:, :128]) / (1.0 + sums[:, 128:])).astype(BF)
    table = all_of(coarse_mid, "dom")
    inputs = jnp.concatenate([coarse_edges, coarse_mid[coarse_receivers], table[coarse_senders]], -1)
    new = coarse_edges.astype(F32) + perceptron(inputs, edge_in[1], mlp_out[2])
    agg = jax.ops.segment_sum(new, coarse_receivers, num_segments=own).astype(BF)
    out = perceptron(jnp.concatenate([coarse_mid, agg], -1), node_in[1], mlp_out[3])
    coarse_out = (coarse_mid.astype(F32) + out).astype(BF)
    above = all_of(coarse_out, "dom")[parents]
    back = perceptron(jnp.concatenate([mid, above], -1), node_in[2], mlp_out[4])
    return (mid.astype(F32) + back).astype(BF), coarse_out


def per_device(
    fine_nodes, fine_edges, fine_senders, fine_receivers, edge_count, ghost_send, fine_parent, coarse_nodes,
    coarse_edges, coarse_senders, coarse_receivers, edge_in, node_in, mlp_out,
):
    groups = lax.axis_size("grp")
    local, parents = fine_nodes[0], fine_parent[0]
    ghosts, place, cplace, pool, ask, flag = early_step(local, ghost_send[0], parents, coarse_senders, groups)
    mid = fine_step(
        edge_count, fine_edges[0], fine_senders[0], fine_receivers[0], local, ghosts.reshape(-1, 128),
        edge_in, node_in, mlp_out,
    )

    def listed_step():
        return late_step(
            mid, place, cplace, pool, ask, coarse_nodes, coarse_edges, coarse_receivers, edge_in, node_in, mlp_out
        )

    def whole_step():
        return dense_step(
            mid, parents, coarse_nodes, coarse_edges, coarse_senders, coarse_receivers, edge_in, node_in, mlp_out
        )

    fine_out, coarse_out = lax.cond(flag[0, 0] > 0, whole_step, listed_step)
    return (fine_out[None], coarse_out)


def solution(mesh):
    fine, coarse = P("grp", "dom"), P("dom")
    in_specs = (fine,) * 7 + (coarse,) * 4 + (P(),) * 3
    return jax.shard_map(
        per_device, mesh=mesh, in_specs=in_specs, out_specs=(fine, coarse), check_vma=False
    )
```

time: 496 us -> 103 us (0.21)
  waiting for transfers between devices: 139 us -> 0 us
  local copies, waits for them, and re-layouts: 130 us -> 2.96 us
  other arithmetic: 120 us -> 0 us
  Pallas kernels: 0 us -> 98.1 us
  blocking collectives: 52.4 us -> 0 us
  starting transfers between devices: 24.2 us -> 0 us
  matrix products: 14 us -> 0 us
  between operations: 14.9 us -> 1.48 us
    scatter-add x4 -> x0, other arithmetic: 102 us -> none  [the longest x1 61 us: per_device(): jax.ops.segment_sum(edge_new * live[:, None], receivers, num_segments=nod...]
    gather x9 -> x0, local copies, waits for them, and re-layouts: 98.6 us -> none  [the longest x2 29.5 us: per_device(): local[receivers]]
    pallas_call x0 -> x3, Pallas kernels: none -> 98.1 us  [the longest x1 56 us: late_step(): pl.pallas_call(late_kernel, name='late', out_shape=[jax.ShapeDtypeStruct(...]
    all_gather x2 -> x0, waiting for transfers between devices: 91.5 us -> none  [gather_in_order(): blocks = lax.all_gather(blocks, axes[k], axis=0, tiled=True)]
    reduce_scatter x2 -> x0, waiting for transfers between devices: 38.6 us -> none  [the longest x1 38.5 us: per_device(): lax.psum_scatter(pooled.astype(jnp.bfloat16), 'grp', scatter_dimension=0,...]
    all_to_all x1 -> x0, blocking collectives: 30.8 us -> none  [summed_on_arrival(): lax.all_to_all(in_blocks(array, dim, peers), axis, 0, 0, tiled=True)]
    all_to_all x2 -> x0, starting transfers between devices: 23.9 us -> none  [the longest x1 12 us: copy_for_each(): lax.all_to_all(jnp.broadcast_to(array[None], (peers, *array.shape)), axis...]
    all_gather x2 -> x0, blocking collectives: 21.5 us -> none  [gather_in_order(): blocks = lax.all_gather(blocks, axes[k], axis=0, tiled=True)]
  transfers between devices with their start and end apart: 6 -> 0, of which waited for: 4 -> 0; matrix products, arithmetic and copies ran while one was open for 38% -> 0% of each run, Pallas kernels for 0% -> 0%
where the time goes in v1:
time: 103 us
  Pallas kernels  98.1 us (95%)
  local copies, waits for them, and re-layouts  2.96 us (3%)
  between operations  1.48 us (1%)
    pallas_call x1, Pallas kernels, late_step(): pl.pallas_call(late_kernel, name='late', out_shape=[jax.ShapeDtypeStruct(...  56 us
    pallas_call x1, Pallas kernels, early_step(): pl.pallas_call(early_kernel, name='early', out_shape=[jax.ShapeDtypeStruc...  22.2 us
    pallas_call x1, Pallas kernels, fine_step(): pl.pallas_call(functools.partial(fine_kernel, block), grid=(steps,), name...  19.9 us
    unnamed x21, local copies, waits for them, and re-layouts  2.28 us

profile of v1, /device:TPU:1, one launch (start us, length us, event | category | flops | bytes accessed | tf_op | source)
XLA Modules:
  0.0 103.0 jit_solution(6480396058276076858)
XLA Ops:
  0.6 0.0 copy-start.16
  0.6 0.0 copy-start.17
  0.7 0.0 copy-start.5
  0.7 0.0 copy-start.7
  0.7 0.0 copy-start.10
  0.7 0.0 copy-start.14
  0.7 0.0 copy-start
  0.7 0.0 copy-start.15
  0.7 0.9 copy.52
  1.6 0.7 reshape_squeeze.9.ghost_ids
  2.3 22.2 %early.1 = (bf16[32,24,128]{2,1,0:T(8,128)(2,1)}, s32[1,768]{1,0:T(1,128)S(1)}, s32[1,512]{1,0:T(1,128)S(1)}, s32[8,128]{1,0:T(8,128)S(1)}, s32[16,128]{1,0:T(8,128)S(1)}, /*index=5*/s32[1,128]{1,0:T(1,128)}) custom-call(bf16[768,128]{1,0:T(8,128)(2,1)} %bitcast.56, s32[1,768]{1,0:T(1,128)} %reshape_squeeze.9.ghost_ids, s32[1,768]{1,0:T(1,128)} %parents.1, ...), custom_call_target="tpu_custom_call" | custom-call | tf_op jit(solution)/shard_map/early/pallas_call | solution.py:266
  24.5 0.0 copy-start.18
  25.1 19.9 %fine_edges.1 = bf16[768,128]{1,0:T(8,128)(2,1)S(1)} custom-call(s32[1,1]{1,0:T(1,128)S(6)} %copy.67.count, bf16[9216,128]{1,0:T(8,128)(2,1)} %bitcast.54, s32[9,1,1024]{2,1,0:T(1,128)} %bitcast.62, s32[9,1,1024]{2,1,0:T(1,128)} %bitcast.63, bf16[768,128]{1,0:T(8,128)(2,1)} %bitcast.57, bf16[768,128]{1,0:T(8,128)(2,1)} %bitcast.59, ...), custom_call_target="tpu_custom_call" | custom-call | tf_op jit(solution)/shard_map/fine_edges/pallas_call | solution.py:124
  45.1 0.0 copy-done.18
  45.1 0.0 copy-done.16
  45.1 0.0 copy-done.17
  45.1 0.0 copy-done.5
  45.1 0.0 copy-done.7
  45.1 0.0 copy-done.10
  45.2 0.0 copy-done.14
  45.2 0.0 copy-done
  45.2 0.0 copy-done.15
  45.2 56.5 %conditional.1 = (bf16[512,128]{1,0:T(8,128)(2,1)S(1)}, bf16[768,128]{1,0:T(8,128)(2,1)S(1)}) conditional(s32[]{:T(128)} %bitcast.15, (s32[4096]{0:T(1024)S(1)}, bf16[768,128]{1,0:T(8,128)(2,1)S(1)}, s32[1,768]{1,0:T(1,128)S(1)}, s32[1,512]{1,0:T(1,128)S(1)}, s32[8,128]{1,0:T(8,128)S(1)}, /*index=5*/s32[16,128]{1,0:T(8,128)S(1)}, ...), branch_computations={%region_0.0_spmd, %region_1.12_spmd} | conditional | flops 687890944 | bytes 189713808 | solution.py:493
  45.4 56.0 %late.1 = (bf16[768,128]{1,0:T(8,128)(2,1)S(1)}, bf16[512,128]{1,0:T(8,128)(2,1)S(1)}) custom-call(bf16[768,128]{1,0:T(8,128)(2,1)S(1)} %get-tuple-element.47.mid_ref, s32[1,768]{1,0:T(1,128)S(1)} %get-tuple-element.48.place_ref, s32[1,512]{1,0:T(1,128)S(1)} %get-tuple-element.49.cplace_ref, s32[8,128]{1,0:T(8,128)S(1)} %get-tuple-element.50.pool_ref, ...), custom_call_target="tpu_custom_call" | custom-call | tf_op jit(solution)/shard_map/cond/branch_0_fun/late/pallas_call | solution.py:403
  101.7 0.7 copy.68
  102.4 0.7 copy.69
Async XLA Ops:
  0.6 44.5 %copy-start.16 = (s32[4096]{0:T(1024)S(1)}, s32[4096]{0:T(1024)}, u32[]{:S(2)}) copy-start(s32[4096]{0:T(1024)} %param.25) | copy-start | bytes 49156
  0.6 44.5 %copy-start.17 = (s32[1,768]{1,0:T(1,128)S(1)}, s32[1,768]{1,0:T(1,128)}, u32[]{:S(2)}) copy-start(s32[1,768]{1,0:T(1,128)} %parents.1) | copy-start | bytes 9220
  0.7 44.5 %copy-start.5 = (bf16[2,384,128]{2,1,0:T(8,128)(2,1)S(1)}, bf16[2,384,128]{2,1,0:T(8,128)(2,1)}, u32[]{:S(2)}) copy-start(bf16[2,384,128]{2,1,0:T(8,128)(2,1)} %ein_ref.1) | copy-start | bytes 589828
  0.7 44.5 %copy-start.7 = (bf16[3,256,128]{2,1,0:T(8,128)(2,1)S(1)}, bf16[3,256,128]{2,1,0:T(8,128)(2,1)}, u32[]{:S(2)}) copy-start(bf16[3,256,128]{2,1,0:T(8,128)(2,1)} %nin_ref.1) | copy-start | bytes 589828
  0.7 44.5 %copy-start.10 = (bf16[5,128,128]{2,1,0:T(8,128)(2,1)S(1)}, bf16[5,128,128]{2,1,0:T(8,128)(2,1)}, u32[]{:S(2)}) copy-start(bf16[5,128,128]{2,1,0:T(8,128)(2,1)} %out_w.1) | copy-start | bytes 491524
  0.7 44.5 %copy-start.14 = (bf16[512,128]{1,0:T(8,128)(2,1)S(1)}, bf16[512,128]{1,0:T(8,128)(2,1)}, u32[]{:S(2)}) copy-start(bf16[512,128]{1,0:T(8,128)(2,1)} %param.23) | copy-start | bytes 393220
  0.7 44.5 %copy-start = (bf16[4096,128]{1,0:T(8,128)(2,1)S(1)}, bf16[4096,128]{1,0:T(8,128)(2,1)}, u32[]{:S(2)}) copy-start(bf16[4096,128]{1,0:T(8,128)(2,1)} %param.24) | copy-start | bytes 3145732
  0.7 44.5 %copy-start.15 = (s32[4096]{0:T(1024)S(1)}, s32[4096]{0:T(1024)}, u32[]{:S(2)}) copy-start(s32[4096]{0:T(1024)} %param.26) | copy-start | bytes 49156
  24.5 20.6 %copy-start.18 = (s32[1,128]{1,0:T(1,128)S(1)}, s32[1,128]{1,0:T(1,128)}, u32[]{:S(2)}) copy-start(s32[1,128]{1,0:T(1,128)} %get-tuple-element.79) | copy-start | bytes 1540

commit v2 on v1

v2 whole, which is shorter than its diff:
```python
import functools

import jax
import jax.numpy as jnp
from jax import lax
from jax.experimental import pallas as pl
from jax.experimental.pallas import tpu as pltpu
from jax.sharding import PartitionSpec as P

BF = jnp.bfloat16
F32 = jnp.float32
I32 = jnp.int32
POOL = 24
POOL_PAD = 32
ASK = 24
AXIS_SHAPE = {"dom": (4, 8), "grp": (4, 2)}
BLOCK = 1024
EARLY_BLOCKS = 4
NT = (((1,), (1,)), ((), ()))


def dot(a, b):
    return jnp.dot(a, b, preferred_element_type=F32)


def iota(shape, axis):
    return lax.broadcasted_iota(I32, shape, axis)


def as_bf(mask):
    return jnp.where(mask, 1.0, 0.0).astype(BF)


def column(row):
    n = row.shape[1]
    return jnp.concatenate(
        [jnp.broadcast_to(row[:, k : k + 128], (128, 128)).T for k in range(0, n, 128)], 0
    )


def pick_rows(col, width):
    n = col.shape[0]
    lane = iota((n, 128), 1)
    return jnp.concatenate([as_bf(col == lane + k) for k in range(0, width, 128)], 1)


def pick_into(row, height, first=0):
    return as_bf(iota((height, row.shape[1]), 0) + first == row)


def mean_of(w):
    mean = jnp.mean(w.astype(F32), axis=1, keepdims=True)
    return jnp.concatenate([w, jnp.broadcast_to(mean, w.shape).astype(BF)], axis=1)


def averager():
    return jnp.full((128, 128), 1.0 / 128, BF)


def second(x, w_mean, ones):
    hidden = (x / (1.0 + jnp.exp(-x))).astype(BF)
    y = dot(hidden, w_mean)
    centre = y[:, :128] - y[:, 128:]
    spread = dot((centre * centre).astype(BF), ones)
    return centre * lax.rsqrt(spread + 1e-5)


def vmem(n):
    return [pl.BlockSpec(memory_space=pltpu.VMEM)] * n


def each_peer(axis, body):
    rows, columns = AXIS_SHAPE[axis]
    me = lax.axis_index(axis)
    row, column_ = me // columns, lax.rem(me, columns)
    wrapped = lambda d, n: min(d, n - d)
    steps = [(r, c) for r in range(rows) for c in range(columns) if r or c]
    steps.sort(key=lambda s: -wrapped(s[0], rows) - wrapped(s[1], columns))
    for r, c in steps:
        body(lax.rem(row + r, rows) * columns + lax.rem(column_ + c, columns))


def greet(axes):
    barrier = pltpu.get_barrier_semaphore()
    for axis in axes:
        each_peer(axis, lambda peer, axis=axis: pl.semaphore_signal(barrier, inc=1, device_id={axis: peer}))


def all_here(axes):
    pl.semaphore_wait(pltpu.get_barrier_semaphore(), sum(lax.axis_size(axis) - 1 for axis in axes))


def send(axis, source, target, sems):
    me = lax.axis_index(axis)

    def one(peer):
        pltpu.make_async_remote_copy(
            src_ref=source(peer), dst_ref=target(me), send_sem=sems.at[0], recv_sem=sems.at[1],
            device_id={axis: peer},
        ).start()

    each_peer(axis, one)


def arrived(axis, span, sems):
    peer = lax.rem(lax.axis_index(axis) + 1, lax.axis_size(axis))
    whole = pltpu.make_async_remote_copy(
        src_ref=span, dst_ref=span, send_sem=sems.at[0], recv_sem=sems.at[1], device_id={axis: peer}
    )
    whole.wait()


def ranked(owner, owners):
    n = owner.shape[1]
    theirs = iota((owners, n), 0) == owner
    before = as_bf(iota((n, n), 0) < iota((n, n), 1))
    counts = dot(as_bf(theirs), before)
    return jnp.sum(jnp.where(theirs, counts, 0.0), axis=0, keepdims=True).astype(I32), theirs


def listed(theirs, value, lane):
    n = value.shape[1]
    code = value + 1
    low, high = (code & 255).astype(F32), (code >> 8).astype(F32)
    parts = jnp.concatenate([jnp.where(theirs, low, 0.0), jnp.where(theirs, high, 0.0)], 0)
    there = as_bf(iota((128, n), 0) == lane)
    out = lax.dot_general(parts.astype(BF), there, NT, preferred_element_type=F32)
    owners = theirs.shape[0]
    return (out[:owners] + 256.0 * out[owners:]).astype(I32)


def step_kernel(
    count_ref, edges_hbm, snd_ref, rcv_ref, local_ref, ghost_ids, parents, csenders, cnodes_ref, cedges_hbm,
    crecv_ref, ein_ref, nin_ref, out_w,
    fine_out, coarse_out, mid_out, flag_out,
    edges, partial, by_sender, by_receiver, total, w_mean, cedges,
    ghost_tx, ghost_rx, note_tx, note_rx, flag_tx, flag_rx,
    up_tx, up_rx, count_tx, count_rx, part_tx, part_rx, cmid, ask_tx, ask_rx, cpart_tx, cpart_rx, cout,
    down_tx, down_rx, ask_sel, down_sel, fsel, cedge, cto, fetch_sems, sems,
):
    me, grp = lax.axis_index("dom"), lax.axis_index("grp")
    peers, groups = lax.axis_size("dom"), lax.axis_size("grp")
    others, friends = peers - 1, groups - 1
    nodes = local_ref.shape[0]
    half = nodes // 2
    blocks, _, block = snd_ref.shape
    own = cnodes_ref.shape[0]
    shift = own.bit_length() - 1
    piece = own // groups
    rows = ghost_tx.shape[1]
    ups, asks = peers * POOL_PAD, peers * ASK
    few, some = pl.ds(0, POOL), pl.ds(0, ASK)
    ones = averager()

    fetch = pltpu.make_async_copy(edges_hbm, edges, fetch_sems.at[0])
    fetch.start()
    cfetch = pltpu.make_async_copy(cedges_hbm, cedges, fetch_sems.at[1])
    cfetch.start()
    up_rx[...] = jnp.zeros_like(up_rx)
    down_rx[...] = jnp.zeros_like(down_rx)
    greet(("dom", "grp"))

    local = local_ref[...]
    picks = dot(pick_rows(column(ghost_ids[...]), nodes), local)
    for p in range(peers):
        ghost_tx[p] = picks[p * rows : (p + 1) * rows].astype(BF)
    parent = parents[...]
    owner, within = parent >> shift, parent & (own - 1)
    rank, theirs = ranked(owner, peers)
    away = owner != me
    place = jnp.where(away, own + owner * POOL_PAD + rank, within)
    excess = jnp.max(jnp.where(away & (rank >= POOL), 1, 0), axis=1, keepdims=True)
    note = listed(theirs, within, rank + lax.rem(me, 4) * POOL_PAD)
    for p in range(peers):
        note_tx[p, :, 0:128] = note[p : p + 1]
    chunk = csenders.shape[1]
    before = as_bf(iota((chunk, chunk), 0) < iota((chunk, chunk), 1))
    senders = csenders[...]
    owners, withins = senders >> shift, senders & (own - 1)
    theirs = [iota((peers, chunk), 0) == owners[k : k + 1] for k in range(groups)]
    counts = dot(jnp.concatenate([as_bf(t) for t in theirs], 0), before)
    past = jnp.zeros((peers, 1), F32)
    cslots, lists, lanes = [], [], []
    for k in range(groups):
        count = counts[k * peers : (k + 1) * peers] + past
        rank = jnp.sum(jnp.where(theirs[k], count, 0.0), axis=0, keepdims=True).astype(I32)
        past = past + jnp.sum(jnp.where(theirs[k], 1.0, 0.0), axis=1, keepdims=True)
        mine, place_ = lax.rem(rank, groups) == grp, rank // groups
        cslots.append(jnp.where(mine & (place_ < ASK), owners[k : k + 1] * ASK + place_, -1))
        lists.append(theirs[k] & mine)
        lanes.append(place_ + lax.rem(me, 4) * POOL_PAD)
    full = jnp.max(past, axis=0, keepdims=True) > float(groups * ASK)
    excess = jnp.maximum(excess, jnp.where(full, 1, 0))
    joined = lambda parts: jnp.concatenate(parts, 1)
    note = listed(joined(lists), joined([withins[k : k + 1] for k in range(groups)]), joined(lanes))
    for p in range(peers):
        note_tx[p, :, 128:256] = note[p : p + 1]
    flag_tx[...] = jnp.broadcast_to(excess, (1, 128))

    w_mean[0] = mean_of(out_w[0])
    w_mean[1] = mean_of(out_w[1])
    by_sender[:, :128] = dot(local, ein_ref[0, 256:384, :]).astype(BF)
    mine = dot(local, ein_ref[0, 128:256, :]).astype(BF)
    by_receiver[:, :128] = mine[:half]
    by_receiver[:, 128:] = mine[half:]
    total[...] = jnp.zeros_like(total)
    fetch.wait()

    def first_part(i, carry):
        at = pl.ds(pl.multiple_of(i * block, block), block)
        rcol = column(rcv_ref[i])
        upper = rcol >= half
        from_r = dot(pick_rows(jnp.where(upper, rcol - half, rcol), half), by_receiver[...])
        partial[at, :] = dot(edges[at, :], ein_ref[0, 0:128, :]) + jnp.where(upper, from_r[:, 128:], from_r[:, :128])
        return carry

    early = EARLY_BLOCKS
    lax.fori_loop(0, early, first_part, 0)
    all_here(("dom", "grp"))
    send("dom", lambda p: ghost_tx.at[p], lambda m: ghost_rx.at[m], sems.at[8])
    send("grp", lambda p: flag_tx, lambda m: flag_rx.at[m], sems.at[9])
    ghost_rx[me] = ghost_tx[me]
    flag_rx[grp] = flag_tx[...]
    lax.fori_loop(early, blocks, first_part, 0)
    cfetch.wait()
    gathered = jnp.zeros((asks, 256), F32)
    lane = iota((chunk, 128), 1)
    for k in range(groups):
        to = column(crecv_ref[k : k + 1])
        facts = jnp.where(lane == 0, to & 255, jnp.where(lane == 1, to >> 8, jnp.where(lane == 2, 1, 0)))
        data = jnp.concatenate([cedges[k * chunk : (k + 1) * chunk], facts.astype(F32).astype(BF)], 1)
        gathered += dot(pick_into(cslots[k], asks), data)
    cedge[...] = gathered[:, :128].astype(BF)
    to = gathered[:, 128:129] + 256.0 * gathered[:, 129:130] + (gathered[:, 130:131] - 1.0)
    cto[...] = jnp.broadcast_to(to, (asks, 128)).astype(I32)
    fsel[...] = pick_rows(column(place), own + ups)
    arrived("grp", flag_rx.at[pl.ds(0, friends)], sems.at[9])
    flag = flag_rx[0]
    for k in range(1, groups):
        flag = jnp.maximum(flag, flag_rx[k])
    for p in range(peers):
        note_tx[p, :, 256:384] = flag
    arrived("dom", ghost_rx.at[pl.ds(0, others)], sems.at[8])
    send("dom", lambda p: note_tx.at[p], lambda m: note_rx.at[m], sems.at[10])
    note_rx[me] = jnp.concatenate([jnp.zeros((1, 128), I32), note_tx[me, :, 128:384]], 1)

    ghosts = ghost_rx[...].astype(F32).reshape(nodes, 128).astype(BF)
    by_sender[:, 128:] = dot(ghosts, ein_ref[0, 256:384, :]).astype(BF)

    def second_part(i, carry):
        at = pl.ds(pl.multiple_of(i * block, block), block)
        receivers = rcv_ref[i]
        scol, rcol = column(snd_ref[i]), column(receivers)
        s_upper, r_upper = scol >= nodes, rcol >= half
        from_s = dot(pick_rows(jnp.where(s_upper, scol - nodes, scol), nodes), by_sender[...])
        x = partial[at, :] + jnp.where(s_upper, from_s[:, 128:], from_s[:, :128])
        new = edges[at, :].astype(F32) + second(x, w_mean[0], ones)
        sides = jnp.concatenate([jnp.where(r_upper, 0.0, new), jnp.where(r_upper, new, 0.0)], 1)
        slot = i * block + iota((1, block), 1)
        into = jnp.where(receivers >= half, receivers - half, receivers)
        into = jnp.where(slot < count_ref[...], into, -1)
        total[...] += dot(pick_into(into, half), sides.astype(BF))
        return carry

    lax.fori_loop(0, blocks, second_part, 0)
    agg = jnp.concatenate([total[:, :128], total[:, 128:]], 0).astype(BF)
    x = dot(local, nin_ref[0, 0:128, :]) + dot(agg, nin_ref[0, 128:256, :])
    mid = (local.astype(F32) + second(x, w_mean[1], ones)).astype(BF)

    up_tx[...] = dot(pick_into(place, ups, own), mid).astype(BF).reshape(up_tx.shape)
    send("dom", lambda p: up_tx.at[p, few], lambda m: up_rx.at[m, few], sems.at[0])
    mid_out[...] = mid

    arrived("dom", note_rx.at[pl.ds(0, others)], sems.at[10])
    flag = note_rx[0, :, 256:384]
    for p in range(1, peers):
        flag = jnp.maximum(flag, note_rx[p, :, 256:384])
    flag_out[...] = flag
    pool_rows = [sum(note_rx[p, :, 0:128] for p in range(k, k + 4)) - 1 for k in range(0, peers, 4)]
    ask_rows = [sum(note_rx[p, :, 128:256] for p in range(k, k + 4)) - 1 for k in range(0, peers, 4)]
    here = pick_into(place, own)
    there = pick_into(jnp.concatenate(pool_rows, 1), own)
    counts = lax.dot_general(jnp.full((8, nodes), 1.0, BF), here, NT, preferred_element_type=F32)
    counts += lax.dot_general(jnp.full((8, ups), 1.0, BF), there, NT, preferred_element_type=F32)
    count_tx[...] = counts[0:1]
    send("grp", lambda p: count_tx, lambda m: count_rx.at[m], sems.at[1])
    count_rx[grp] = count_tx[...]
    pooled = dot(here, mid)
    for k, row in enumerate(ask_rows):
        ask_sel[128 * k : 128 * (k + 1), :] = pick_rows(column(row), own)
    for k, row in enumerate(pool_rows):
        down_sel[128 * k : 128 * (k + 1), :] = pick_rows(column(row), own)
    to = cto[...]
    from_r = pick_rows(to, own)
    into = pick_into(jnp.concatenate([to[k : k + 128].T[0:1] for k in range(0, asks, 128)], 1), own)
    w_edge, w_node, w_back = mean_of(out_w[2]), mean_of(out_w[3]), mean_of(out_w[4])
    arrived("grp", count_rx.at[pl.ds(0, friends)], sems.at[1])
    children = count_rx[0]
    for k in range(1, groups):
        children = children + count_rx[k]
    diagonal = iota((piece, own), 1) == iota((piece, own), 0) + grp * piece
    children = jnp.sum(jnp.where(diagonal, children, 0.0), axis=1, keepdims=True)

    arrived("dom", up_rx.at[pl.ds(0, others), few], sems.at[0])
    pooled += dot(there, up_rx[...].reshape(ups, 128))
    part_tx[...] = pooled.astype(BF).reshape(part_tx.shape)
    send("grp", lambda p: part_tx.at[p], lambda m: part_rx.at[m], sems.at[2])
    part_rx[grp] = part_tx[grp]
    arrived("grp", part_rx.at[pl.ds(0, friends)], sems.at[2])
    mine = pl.ds(pl.multiple_of(grp * piece, piece), piece)
    sums = cnodes_ref[mine, :].astype(F32)
    for k in range(groups):
        sums = sums + part_rx[k].astype(F32)
    own_mid = (sums / (1.0 + children)).astype(BF)
    cmid[grp] = own_mid
    send("grp", lambda p: cmid.at[grp], lambda m: cmid.at[m], sems.at[3])
    arrived("grp", cmid.at[pl.ds(0, friends)], sems.at[3])

    coarse = cmid[...].reshape(own, 128)
    ask_tx[...] = dot(ask_sel[...], coarse).astype(BF).reshape(ask_tx.shape)
    send("dom", lambda p: ask_tx.at[p, some], lambda m: ask_rx.at[m], sems.at[4])
    ask_rx[me] = ask_tx[me, 0:ASK]
    edge = cedge[...]
    x = dot(edge, ein_ref[1, 0:128, :]) + dot(dot(from_r, coarse).astype(BF), ein_ref[1, 128:256, :])
    arrived("dom", ask_rx.at[pl.ds(0, others)], sems.at[4])
    x += dot(ask_rx[...].astype(F32).reshape(asks, 128).astype(BF), ein_ref[1, 256:384, :])
    new = edge.astype(F32) + second(x, w_edge, ones)
    cpart_tx[...] = dot(into, new.astype(BF)).astype(BF).reshape(cpart_tx.shape)
    send("grp", lambda p: cpart_tx.at[p], lambda m: cpart_rx.at[m], sems.at[5])
    cpart_rx[grp] = cpart_tx[grp]
    x = dot(own_mid, nin_ref[1, 0:128, :])
    arrived("grp", cpart_rx.at[pl.ds(0, friends)], sems.at[5])
    sums = cpart_rx[0].astype(F32)
    for k in range(1, groups):
        sums = sums + cpart_rx[k].astype(F32)
    x += dot(sums.astype(BF), nin_ref[1, 128:256, :])
    cout[grp] = (own_mid.astype(F32) + second(x, w_node, ones)).astype(BF)
    send("grp", lambda p: cout.at[grp], lambda m: cout.at[m], sems.at[6])
    arrived("grp", cout.at[pl.ds(0, friends)], sems.at[6])

    coarse = cout[...].reshape(own, 128)
    down_tx[...] = dot(down_sel[...], coarse).astype(BF).reshape(down_tx.shape)
    send("dom", lambda p: down_tx.at[p, few], lambda m: down_rx.at[m, few], sems.at[7])
    coarse_out[...] = coarse
    above = dot(fsel[:, 0:own], coarse)
    x = dot(mid, nin_ref[2, 0:128, :])
    arrived("dom", down_rx.at[pl.ds(0, others), few], sems.at[7])
    above += dot(fsel[:, own:], down_rx[...].reshape(ups, 128))
    x += dot(above.astype(BF), nin_ref[2, 128:256, :])
    fine_out[...] = (mid.astype(F32) + second(x, w_back, ones)).astype(BF)


def whole_step(
    count, edges, senders, receivers, local, ghost_send, parents, coarse_nodes, coarse_edges, coarse_senders,
    coarse_receivers, edge_in, node_in, mlp_out,
):
    peers, groups = lax.axis_size("dom"), lax.axis_size("grp")
    own, nodes, slots, rows = coarse_nodes.shape[0], local.shape[0], edges.shape[0], ghost_send.shape[1]
    nedges, piece = coarse_edges.shape[0], own // groups
    blocks = slots // BLOCK
    buffer = lambda *shape: pltpu.VMEM(shape, BF)
    pair = lambda *shape: [buffer(*shape), buffer(*shape)]
    anywhere = [pl.BlockSpec(memory_space=pl.ANY)]
    return pl.pallas_call(
        step_kernel,
        name="step",
        out_shape=[
            jax.ShapeDtypeStruct((nodes, 128), BF), jax.ShapeDtypeStruct((own, 128), BF),
            jax.ShapeDtypeStruct((nodes, 128), BF), jax.ShapeDtypeStruct((1, 128), I32),
        ],
        in_specs=vmem(1) + anywhere + vmem(7) + anywhere + vmem(4),
        out_specs=vmem(4),
        scratch_shapes=[
            buffer(slots, 128), pltpu.VMEM((slots, 128), F32), buffer(nodes, 256), buffer(nodes // 2, 256),
            pltpu.VMEM((nodes // 2, 256), F32), buffer(2, 128, 256), buffer(nedges, 128),
            *pair(peers, rows, 128),
            pltpu.VMEM((peers, 1, 384), I32), pltpu.VMEM((peers, 1, 384), I32),
            pltpu.VMEM((1, 128), I32), pltpu.VMEM((groups, 1, 128), I32),
            *pair(peers, POOL_PAD, 128),
            pltpu.VMEM((1, own), F32), pltpu.VMEM((groups, 1, own), F32),
            *pair(groups, piece, 128), buffer(groups, piece, 128),
            buffer(peers, POOL_PAD, 128), buffer(peers, ASK, 128),
            *pair(groups, piece, 128), buffer(groups, piece, 128),
            *pair(peers, POOL_PAD, 128),
            buffer(peers * POOL_PAD, own), buffer(peers * POOL_PAD, own),
            buffer(nodes, own + peers * POOL_PAD), buffer(peers * ASK, 128), pltpu.VMEM((peers * ASK, 128), I32),
            pltpu.SemaphoreType.DMA((2,)), pltpu.SemaphoreType.DMA((11, 2)),
        ],
        compiler_params=pltpu.CompilerParams(collective_id=0, has_side_effects=True),
    )(
        count, edges, senders.reshape(blocks, 1, BLOCK), receivers.reshape(blocks, 1, BLOCK), local,
        ghost_send.reshape(1, -1), parents.reshape(1, -1), coarse_senders.reshape(groups, -1),
        coarse_nodes, coarse_edges, coarse_receivers.reshape(groups, -1), edge_in, node_in, mlp_out,
    )


def layer_norm(values):
    centre = values - jnp.mean(values, -1, keepdims=True)
    spread = jnp.mean(centre * centre, -1, keepdims=True)
    return centre * lax.rsqrt(spread + 1e-05)


def perceptron(inputs, w_first, w_second):
    hidden = jax.nn.silu(jnp.dot(inputs, w_first, preferred_element_type=F32)).astype(BF)
    return layer_norm(jnp.dot(hidden, w_second, preferred_element_type=F32))


def summed(array, axis):
    return jnp.sum(lax.all_to_all(array, axis, 0, 0, tiled=True), axis=0)


def all_of(array, axis):
    peers = lax.axis_size(axis)
    copies = lax.all_to_all(jnp.broadcast_to(array[None], (peers, *array.shape)), axis, 0, 0, tiled=True)
    return copies.reshape(peers * array.shape[0], *array.shape[1:])


def dense_step(
    mid, parents, coarse_nodes, coarse_edges, coarse_senders, coarse_receivers, edge_in, node_in, mlp_out
):
    peers, groups = lax.axis_size("dom"), lax.axis_size("grp")
    own = coarse_nodes.shape[0]
    piece = own // groups
    wide = jnp.concatenate([mid.astype(F32), jnp.ones(mid.shape, F32)], -1)
    sums = jax.ops.segment_sum(wide, parents, num_segments=own * peers)
    sums = jnp.moveaxis(sums.reshape(peers, groups, piece, 256), 1, 0)
    sums = all_of(summed(summed(sums, "grp"), "dom"), "grp")
    coarse_mid = ((coarse_nodes.astype(F32) + sums[:, :128]) / (1.0 + sums[:, 128:])).astype(BF)
    table = all_of(coarse_mid, "dom")
    inputs = jnp.concatenate([coarse_edges, coarse_mid[coarse_receivers], table[coarse_senders]], -1)
    new = coarse_edges.astype(F32) + perceptron(inputs, edge_in[1], mlp_out[2])
    agg = jax.ops.segment_sum(new, coarse_receivers, num_segments=own).astype(BF)
    out = perceptron(jnp.concatenate([coarse_mid, agg], -1), node_in[1], mlp_out[3])
    coarse_out = (coarse_mid.astype(F32) + out).astype(BF)
    above = all_of(coarse_out, "dom")[parents]
    back = perceptron(jnp.concatenate([mid, above], -1), node_in[2], mlp_out[4])
    return (mid.astype(F32) + back).astype(BF), coarse_out


def per_device(
    fine_nodes, fine_edges, fine_senders, fine_receivers, edge_count, ghost_send, fine_parent, coarse_nodes,
    coarse_edges, coarse_senders, coarse_receivers, edge_in, node_in, mlp_out,
):
    parents = fine_parent[0]
    fine_out, coarse_out, mid, flag = whole_step(
        edge_count, fine_edges[0], fine_senders[0], fine_receivers[0], fine_nodes[0], ghost_send[0], parents,
        coarse_nodes, coarse_edges, coarse_senders, coarse_receivers, edge_in, node_in, mlp_out,
    )

    def again():
        return dense_step(
            mid, parents, coarse_nodes, coarse_edges, coarse_senders, coarse_receivers, edge_in, node_in, mlp_out
        )

    fine_out, coarse_out = lax.cond(flag[0, 0] > 0, again, lambda: (fine_out, coarse_out))
    return (fine_out[None], coarse_out)


def solution(mesh):
    fine, coarse = P("grp", "dom"), P("dom")
    in_specs = (fine,) * 7 + (coarse,) * 4 + (P(),) * 3
    return jax.shard_map(
        per_device, mesh=mesh, in_specs=in_specs, out_specs=(fine, coarse), check_vma=False
    )
```

time: 103 us -> 88.3 us (0.86)
  Pallas kernels: 98.1 us -> 79.9 us
  local copies, waits for them, and re-layouts: 2.96 us -> 6.09 us
    pallas_call x3 -> x1, Pallas kernels: 98.1 us -> 79.9 us  [whole_step(): pl.pallas_call(step_kernel, name='step', out_shape=[jax.ShapeDtypeStruct(...]
    reshape x0 -> x2, local copies, waits for them, and re-layouts: none -> 2.65 us  [the longest x1 1.32 us: whole_step(): coarse_receivers.reshape(groups, -1)]
    unnamed x21 -> x12, local copies, waits for them, and re-layouts: 2.28 us -> 2.45 us
where the time goes in v2:
time: 88.3 us; the launch traced here: 88 us
  Pallas kernels  79.9 us (90%)
  local copies, waits for them, and re-layouts  6.09 us (7%)
  between operations  1.93 us (2%)
    pallas_call x1, Pallas kernels, whole_step(): pl.pallas_call(step_kernel, name='step', out_shape=[jax.ShapeDtypeStruct(...  79.9 us
    unnamed x12, local copies, waits for them, and re-layouts  2.45 us

profile of v2, /device:TPU:1, one launch (start us, length us, event | category | flops | bytes accessed | tf_op | source)
XLA Modules:
  0.0 88.0 jit_solution(2324870686856908545)
XLA Ops:
  0.6 0.8 copy.51
  1.4 0.7 reshape_squeeze.11.ghost_ids
  2.1 1.3 %reshape.84.csenders = s32[8,512]{1,0:T(8,128)} reshape(s32[4096]{0:T(1024)} %param.25) | data formatting | bytes 32768 | tf_op jit(solution)/shard_map/reshape | solution.py:392
  3.4 1.3 %reshape.85.crecv_ref = s32[8,512]{1,0:T(8,128)} reshape(s32[4096]{0:T(1024)} %param.26) | data formatting | bytes 32768 | tf_op jit(solution)/shard_map/reshape | solution.py:393
  5.4 0.0 copy-start
  5.4 0.0 copy-start.2
  5.4 0.0 copy-start.7
  5.4 0.0 copy-start.9
  5.4 79.9 %step.1 = (bf16[768,128]{1,0:T(8,128)(2,1)S(1)}, bf16[512,128]{1,0:T(8,128)(2,1)}, bf16[768,128]{1,0:T(8,128)(2,1)S(1)}, s32[1,128]{1,0:T(1,128)}) custom-call(s32[1,1]{1,0:T(1,128)S(6)} %copy.66.count_ref, bf16[9216,128]{1,0:T(8,128)(2,1)} %bitcast.53, s32[9,1,1024]{2,1,0:T(1,128)} %bitcast.57, s32[9,1,1024]{2,1,0:T(1,128)} %bitcast.58, ...), custom_call_target="tpu_custom_call" | custom-call | tf_op jit(solution)/shard_map/step/pallas_call | solution.py:364
  86.0 0.0 copy-done
  86.0 0.0 copy-done.2
  86.0 0.0 copy-done.7
  86.0 0.0 copy-done.9
  86.0 0.3 conditional.1
  86.0 0.1 copy.52
  86.2 0.2 copy.56
  86.3 0.0 copy-start.6
  86.3 1.6 %copy.67 = bf16[512,128]{1,0:T(8,128)(2,1)} copy(bf16[512,128]{1,0:T(8,128)(2,1)} %get-tuple-element.123) | data formatting | bytes 262144
  88.0 0.0 copy-done.6
Async XLA Ops:
  5.4 80.6 %copy-start = (bf16[4096,128]{1,0:T(8,128)(2,1)S(1)}, bf16[4096,128]{1,0:T(8,128)(2,1)}, u32[]{:S(2)}) copy-start(bf16[4096,128]{1,0:T(8,128)(2,1)} %cedges_hbm.1) | copy-start | bytes 3145732
  5.4 80.6 %copy-start.2 = (bf16[512,128]{1,0:T(8,128)(2,1)S(1)}, bf16[512,128]{1,0:T(8,128)(2,1)}, u32[]{:S(2)}) copy-start(bf16[512,128]{1,0:T(8,128)(2,1)} %cnodes_ref.1) | copy-start | bytes 393220
  5.4 80.6 %copy-start.7 = (s32[4096]{0:T(1024)S(1)}, s32[4096]{0:T(1024)}, u32[]{:S(2)}) copy-start(s32[4096]{0:T(1024)} %param.25) | copy-start | bytes 49156
  5.4 80.5 %copy-start.9 = (s32[1,768]{1,0:T(1,128)S(1)}, s32[1,768]{1,0:T(1,128)}, u32[]{:S(2)}) copy-start(s32[1,768]{1,0:T(1,128)} %parents.1) | copy-start | bytes 9220
  86.3 1.7 %copy-start.6 = (bf16[1,768,128]{2,1,0:T(8,128)(2,1)}, bf16[1,768,128]{2,1,0:T(8,128)(2,1)S(1)}, u32[]{:S(2)}) copy-start(bf16[1,768,128]{2,1,0:T(8,128)(2,1)S(1)} %get-tuple-element.122) | copy-start | bytes 589828
